TPU v7x, 32 devices: a whole 2x2x4 slice. The times are simulated.
32 devices in a mesh: loss: 4 (over x, core), tower: 4 (over z), pipe: 2 (over y).
Axes of the slice: x: 2, y: 2, z: 4, core: 2. Of those that a mesh axis runs over, the one named last changes fastest.
Arguments:
- image_feats: bfloat16 [4, 2, 24, 1536], P('loss', 'pipe', None, 'tower'), may hold values from -6 to 6
- text_tokens: bfloat16 [4, 2, 24, 64, 1152], P('loss', 'pipe', None, None, 'tower'), may hold values from -6 to 6
- lengths: int32 [4, 2, 24], P('loss', 'pipe'), may hold values from 1 to 64, as said below
- w_image: bfloat16 [1536, 1536], P('tower'), may hold values from -0.15625 to 0.15625
- w_text: bfloat16 [1152, 1536], P('tower'), may hold values from -0.1875 to 0.1875
- logit_scale: float32 [1], replicated, may hold values from 24 to 48
- logit_bias: float32 [1], replicated, may hold values from -4 to -2
Outputs:
- image_grad: float32 [4, 2, 24, 1536], P('loss', 'pipe', 'tower')
- text_grad: float32 [4, 2, 24, 1536], P('loss', 'pipe', 'tower')
Inputs may be any that keep to these rules, and one draw needn't show every extreme that they name: `lengths`: in every group of 24 captions one caption has 64 tokens and one has a single token.
All inputs are finite; a program needn't handle non-finite values.
Results may differ from a plain program's by a relative error of at most 0.0036.
The roundings to bfloat16 on the way count: a program that leaves them out, or rounds other values in their place, can miss the bound.
Values may be sent and summed in bfloat16 or wider, within the bound.
A program may use at most 64 MiB of HBM per device.

v0:
```python
import functools

import jax
import jax.numpy as jnp
from jax import lax
from jax.experimental import pallas as pl
from jax.experimental.pallas import tpu as pltpu
from jax.sharding import PartitionSpec as P

MESH = pl.DeviceIdType.MESH
WIRE = jnp.bfloat16
SUM = jnp.float32
F32 = jnp.float32
UNROLL = 16
LANES = 128


def each(lo, hi, body):
    if hi - lo <= UNROLL:
        for k in range(lo, hi):
            body(k)
    else:
        lax.fori_loop(lo, hi, lambda k, c: (body(k), c)[1], 0)


def kernel(
    sub, towers, pipes, planes,
    scale_hbm, shift_hbm, feats_hbm, words_hbm, lens_hbm, wi_hbm, wt_hbm,
    image_out, text_out,
    scale_ref, shift_ref, feats, words, lens, wi, wt,
    part_i, part_t, got_i, got_t, images, texts, term_i, term_t, back_i, back_t,
    flat, load_sem, s1, r1, s2, r2, s3, r3, s4, r4, s5, r5, s6, r6,
):
    pad = -(-sub // 8) * 8
    group, width = feats.shape
    length = words.shape[1]
    emb = wi.shape[1]
    rows = towers * pad
    tower = lax.axis_index("tower")
    plane = lax.axis_index("loss") * pipes + lax.axis_index("pipe")

    def tower_peer(k):
        return {"tower": lax.rem(tower + k, towers)}

    def plane_peer(k):
        q = lax.rem(plane + k, planes)
        return {"loss": q // pipes, "pipe": lax.rem(q, pipes)}

    loads = []
    for n, (src, dst) in enumerate((
        (lens_hbm.at[0], lens),
        (words_hbm.at[0, 0], words),
        (wt_hbm, wt),
        (feats_hbm.at[0, 0], feats),
        (wi_hbm, wi),
        (scale_hbm, scale_ref),
        (shift_hbm, shift_ref),
    )):
        loads.append(pltpu.make_async_copy(src, dst, load_sem.at[n]))
        loads[-1].start()

    barrier = pltpu.get_barrier_semaphore()
    each(1, towers, lambda k: pl.semaphore_signal(
        barrier, inc=1, device_id=tower_peer(k), device_id_type=MESH))
    each(1, planes, lambda k: pl.semaphore_signal(
        barrier, inc=1, device_id=plane_peer(k), device_id_type=MESH))

    def source_row(shape):
        at = lax.broadcasted_iota(jnp.int32, shape, 0)
        r = at % pad
        return jnp.where(r < sub, at // pad * sub + r, -1)

    pick = (source_row((rows, group)) == lax.broadcasted_iota(jnp.int32, (rows, group), 1))

    def scatter(k, part, got, send, recv):
        return pltpu.make_async_remote_copy(
            src_ref=part.at[lax.rem(tower + k, towers)], dst_ref=got.at[k - 1],
            send_sem=send.at[k - 1], recv_sem=recv.at[k - 1],
            device_id=tower_peer(k), device_id_type=MESH)

    def pack(part, raw):
        for d in range(towers):
            for c in range(emb // LANES):
                part[d, c * sub:(c + 1) * sub, :] = raw[
                    d * pad:d * pad + sub, c * LANES:(c + 1) * LANES]

    loads[0].wait()
    counts = jnp.sum(jnp.where(pick, lens[...].astype(F32), 0.0), axis=1, keepdims=True)
    spot = lax.broadcasted_iota(jnp.int32, (rows, group * length), 1)
    first = source_row((rows, group * length)) * length
    keep = (spot >= first) & (spot < first + counts.astype(jnp.int32)) & (first >= 0)
    keep = jnp.where(keep, 1.0, 0.0).astype(jnp.bfloat16)
    loads[1].wait()
    summed = jnp.dot(keep, words[...].reshape(group * length, words.shape[2]),
                     preferred_element_type=F32)
    pooled = (summed / jnp.maximum(counts, 1.0)).astype(jnp.bfloat16)
    loads[2].wait()
    raw_t = jnp.dot(pooled, wt[...], preferred_element_type=F32)
    pack(part_t, raw_t)
    pl.semaphore_wait(barrier, towers + planes - 2)
    each(1, towers, lambda k: scatter(k, part_t, got_t, s1, r1).start())

    loads[3].wait()
    moved = jnp.dot(jnp.where(pick, 1.0, 0.0).astype(jnp.bfloat16), feats[...],
                    preferred_element_type=F32).astype(jnp.bfloat16)
    loads[4].wait()
    raw_i = jnp.dot(moved, wi[...], preferred_element_type=F32)
    pack(part_i, raw_i)
    each(1, towers, lambda k: scatter(k, part_i, got_i, s2, r2).start())

    def padded(x):
        x = x.astype(F32)
        if pad > sub:
            x = jnp.concatenate([x, jnp.zeros((x.shape[0], pad - sub, emb), F32)], axis=1)
        return x.reshape(x.shape[0] * pad, emb).astype(jnp.bfloat16)

    def unit(part, got, send, recv):
        each(1, towers, lambda k: scatter(k, part, got, send, recv).wait_recv())
        raw = part[tower]
        for k in range(towers - 1):
            raw = raw + got[k]
        flat[...] = raw
        raw = jnp.concatenate(
            [flat[c * sub:(c + 1) * sub, :] for c in range(emb // LANES)], axis=1)
        size = jnp.sum(raw * raw, axis=-1, keepdims=True) + 1e-06
        return (raw * lax.rsqrt(size)).astype(jnp.bfloat16)

    def spread_t(k):
        return pltpu.make_async_remote_copy(
            src_ref=texts.at[plane], dst_ref=texts.at[plane],
            send_sem=s3.at[k - 1], recv_sem=r3.at[k - 1],
            device_id=plane_peer(k), device_id_type=MESH)

    def spread_i(k):
        return pltpu.make_async_remote_copy(
            src_ref=images.at[tower], dst_ref=images.at[tower],
            send_sem=s4.at[k - 1], recv_sem=r4.at[k - 1],
            device_id=tower_peer(k), device_id_type=MESH)

    texts[plane] = unit(part_t, got_t, s1, r1)
    each(1, planes, lambda k: spread_t(k).start())
    images[tower] = unit(part_i, got_i, s2, r2)
    each(1, towers, lambda k: spread_i(k).start())
    each(1, planes, lambda k: spread_t(k).wait_recv())
    each(1, towers, lambda k: spread_i(k).wait_recv())

    loads[5].wait()
    loads[6].wait()
    scale = scale_ref[0]
    shift = shift_ref[0]
    cols = planes * pad
    all_i = padded(images[...])
    all_t = padded(texts[...])
    scores = lax.dot_general(all_i, all_t, (((1,), (1,)), ((), ())), preferred_element_type=F32)
    at_i = lax.broadcasted_iota(jnp.int32, (rows, cols), 0) - tower * pad
    at_t = lax.broadcasted_iota(jnp.int32, (rows, cols), 1) - plane * pad
    match = jnp.where((at_i == at_t) & (at_i >= 0) & (at_i < pad), 1.0, 0.0)
    grads = jax.nn.sigmoid(scale * scores + shift) - match

    def back_image(k):
        return pltpu.make_async_remote_copy(
            src_ref=term_i.at[lax.rem(tower + k, towers)], dst_ref=back_i.at[k - 1],
            send_sem=s5.at[k - 1], recv_sem=r5.at[k - 1],
            device_id=tower_peer(k), device_id_type=MESH)

    def back_text(k):
        return pltpu.make_async_remote_copy(
            src_ref=term_t.at[lax.rem(plane + k, planes)], dst_ref=back_t.at[k - 1],
            send_sem=s6.at[k - 1], recv_sem=r6.at[k - 1],
            device_id=plane_peer(k), device_id_type=MESH)

    sums_i = jnp.dot(grads.astype(jnp.bfloat16), all_t, preferred_element_type=F32)
    term_i[...] = sums_i.reshape(towers, pad, emb)[:, :sub].astype(WIRE)
    each(1, towers, lambda k: back_image(k).start())
    grads_t = grads.T.astype(jnp.bfloat16)
    sums_t = jnp.dot(grads_t, all_i, preferred_element_type=F32)
    term_t[...] = sums_t.reshape(planes, pad, emb)[:, :sub].astype(WIRE)
    each(1, planes, lambda k: back_text(k).start())

    mine_t = lax.broadcasted_iota(jnp.int32, (pad, cols), 0) + plane * pad
    mine_t = jnp.where(mine_t == lax.broadcasted_iota(jnp.int32, (pad, cols), 1), 1.0, 0.0)
    mine_i = lax.broadcasted_iota(jnp.int32, (pad, rows), 0) + tower * pad
    mine_i = jnp.where(mine_i == lax.broadcasted_iota(jnp.int32, (pad, rows), 1), 1.0, 0.0)
    own_gt = jnp.dot(mine_t.astype(jnp.bfloat16), grads_t, preferred_element_type=F32)
    own_gi = jnp.dot(mine_i.astype(jnp.bfloat16), grads.astype(jnp.bfloat16),
                     preferred_element_type=F32)
    own_t = jnp.dot(own_gt.astype(jnp.bfloat16), all_i, preferred_element_type=F32)
    own_i = jnp.dot(own_gi.astype(jnp.bfloat16), all_t, preferred_element_type=F32)

    each(1, planes, lambda k: back_text(k).wait_recv())
    text_out[:, 0, :] = (own_t[:sub] + jnp.sum(back_t[...].astype(F32), axis=0))
    each(1, towers, lambda k: back_image(k).wait_recv())
    image_out[:, 0, :] = (own_i[:sub] + jnp.sum(back_i[...].astype(F32), axis=0))

    each(1, towers, lambda k: scatter(k, part_t, got_t, s1, r1).wait_send())
    each(1, towers, lambda k: scatter(k, part_i, got_i, s2, r2).wait_send())
    each(1, planes, lambda k: spread_t(k).wait_send())
    each(1, towers, lambda k: spread_i(k).wait_send())
    each(1, towers, lambda k: back_image(k).wait_send())
    each(1, planes, lambda k: back_text(k).wait_send())


def finish(scale_ref, image_ref, text_ref, image_out, text_out):
    image_out[...] = scale_ref[0] * image_ref[...]
    text_out[...] = scale_ref[0] * text_ref[...]


def per_device(towers, pipes, planes, image_feats, text_tokens, lengths, w_image, w_text,
               logit_scale, logit_bias):
    group = image_feats.shape[2]
    emb = w_image.shape[1]
    sub = group // towers
    out = jax.ShapeDtypeStruct((sub, 1, emb), F32)
    sems = []
    for n in (towers, towers, planes, towers, towers, planes):
        sems += [pltpu.SemaphoreType.DMA((n - 1,))] * 2
    outs = pl.pallas_call(
        functools.partial(kernel, sub, towers, pipes, planes),
        out_shape=(out, out),
        in_specs=[pl.BlockSpec(memory_space=pltpu.HBM)] * 2
        + [pl.BlockSpec(memory_space=pl.ANY)] * 5,
        out_specs=(pl.BlockSpec(memory_space=pltpu.VMEM),) * 2,
        scratch_shapes=[
            pltpu.SMEM(logit_scale.shape, F32),
            pltpu.SMEM(logit_bias.shape, F32),
            pltpu.VMEM(image_feats.shape[2:], image_feats.dtype),
            pltpu.VMEM(text_tokens.shape[2:], text_tokens.dtype),
            pltpu.VMEM(lengths.shape[1:], lengths.dtype),
            pltpu.VMEM(w_image.shape, w_image.dtype),
            pltpu.VMEM(w_text.shape, w_text.dtype),
            pltpu.VMEM((towers, sub * emb // LANES, LANES), SUM),
            pltpu.VMEM((towers, sub * emb // LANES, LANES), SUM),
            pltpu.VMEM((towers - 1, sub * emb // LANES, LANES), SUM),
            pltpu.VMEM((towers - 1, sub * emb // LANES, LANES), SUM),
            pltpu.VMEM((towers, sub, emb), jnp.bfloat16),
            pltpu.VMEM((planes, sub, emb), jnp.bfloat16),
            pltpu.VMEM((towers, sub, emb), WIRE),
            pltpu.VMEM((planes, sub, emb), WIRE),
            pltpu.VMEM((towers - 1, sub, emb), WIRE),
            pltpu.VMEM((planes - 1, sub, emb), WIRE),
            pltpu.VMEM((sub * emb // LANES, LANES), SUM),
            pltpu.SemaphoreType.DMA((7,)),
        ] + sems,
        compiler_params=pltpu.CompilerParams(collective_id=0, has_side_effects=True),
    )(logit_scale, logit_bias, image_feats, text_tokens, lengths, w_image, w_text)
    outs = pl.pallas_call(
        finish,
        out_shape=(out, out),
        in_specs=[pl.BlockSpec(memory_space=pltpu.SMEM)]
        + [pl.BlockSpec(memory_space=pltpu.VMEM)] * 2,
        out_specs=(pl.BlockSpec(memory_space=pltpu.VMEM),) * 2,
    )(logit_scale, *outs)
    return tuple(o.reshape(1, 1, sub, emb) for o in outs)


def solution(mesh):
    shape = dict(mesh.shape)
    planes = shape["loss"] * shape["pipe"]
    return jax.shard_map(
        functools.partial(per_device, shape["tower"], shape["pipe"], planes),
        mesh=mesh,
        in_specs=(
            P("loss", "pipe", None, "tower"),
            P("loss", "pipe", None, None, "tower"),
            P("loss", "pipe", None),
            P("tower", None),
            P("tower", None),
            P(),
            P(),
        ),
        out_specs=(P("loss", "pipe", "tower", None), P("loss", "pipe", "tower", None)),
        check_vma=False,
    )
```

profile of v0, /device:TPU:0, one launch (start us, length us, event | category | flops | bytes accessed | tf_op | source)
XLA Modules:
  0.0 26.7 jit_solution(12218984499779832021)
XLA Ops:
  1.9 23.3 %shard_map.86 = (f32[6,1,1536]{2,1,0:T(1,128)}, f32[6,1,1536]{2,1,0:T(1,128)}) custom-call(f32[1]{0:T(128)S(6)} %copy.11.scale_hbm.scale_ref, f32[1]{0:T(128)S(6)} %copy.12.shift_hbm, bf16[1,1,24,384]{3,2,1,0:T(8,128)(2,1)} %feats_hbm.1, bf16[1,1,24,64,288]{4,3,2,1,0:T(8,128)(2,1)} %words_hbm.1, s32[1,1,24]{2,1,0:T(1,128)} %lens_hbm.1, ...), custom_call_target="tpu_custom_call" | custom-call | tf_op jit(solution)/shard_map/pallas_call | solution.py:217
  25.2 1.4 %shard_map.87 = (f32[6,1,1536]{2,1,0:T(1,128)}, f32[6,1,1536]{2,1,0:T(1,128)}) custom-call(f32[1]{0:T(128)S(6)} %copy.11.scale_hbm.scale_ref, f32[6,1,1536]{2,1,0:T(1,128)} %get-tuple-element.6.image_ref, f32[6,1,1536]{2,1,0:T(1,128)} %get-tuple-element.7.text_ref), custom_call_target="tpu_custom_call" | custom-call | tf_op jit(solution)/shard_map/pallas_call | solution.py:246
where the time goes:
time: 26.9 us; the launch traced here: 26.7 us
  Pallas kernels  24.7 us (92%)
  between operations  1.93 us (7%)
    pallas_call x1, Pallas kernels, per_device(): pl.pallas_call(functools.partial(kernel, sub, towers, pipes, planes), out...  23.3 us
    pallas_call x1, Pallas kernels, per_device(): pl.pallas_call(finish, out_shape=(out, out), in_specs=[pl.BlockSpec(memor...  1.42 us

commit v1 on v0

v1 whole, which is shorter than its diff:
```python
import functools

import jax
import jax.numpy as jnp
from jax import lax
from jax.experimental import pallas as pl
from jax.experimental.pallas import tpu as pltpu
from jax.sharding import PartitionSpec as P

MESH = pl.DeviceIdType.MESH
WIRE = jnp.bfloat16
CODE = jnp.int16
F32 = jnp.float32
BF16 = jnp.bfloat16
UNROLL = 16
LANES = 128
STEPS = 32752.0
LN2 = 0.6931471805599453


def each(lo, hi, body):
    if hi - lo <= UNROLL:
        for k in reversed(range(lo, hi)):
            body(k)
    else:
        lax.fori_loop(lo, hi, lambda k, c: (body(k), c)[1], 0)


def partner(me, k, n):
    if n <= UNROLL and n & (n - 1) == 0:
        q = me
        for b in range(n.bit_length() - 1):
            if (k >> b) & 1:
                q = q + (1 - 2 * lax.rem(me // (1 << b), 2)) * (1 << b)
        return q, q
    return lax.rem(me + k, n), lax.rem(me + n - k, n)


def kernel(
    sub, towers, pipes, planes,
    scale_hbm, shift_hbm, feats_hbm, words_hbm, lens_hbm, wi_hbm, wt_hbm,
    image_out, text_out,
    scale_ref, shift_ref, feats, words, lens, wi, wt,
    flat_i, flat_t, power_i, power_t, part_i, part_t, got_i, got_t, code,
    full_i, full_t, images, texts, sums_i, sums_t, term_i, term_t, back_i, back_t,
    load_sem, s1, r1, s2, r2, s3, r3, s4, r4, s5, r5, s6, r6,
):
    group, width = feats.shape
    length = words.shape[1]
    emb = wi.shape[1]
    chunks = emb // LANES
    rows = sub * chunks
    span = term_i.shape[1]
    tower = lax.axis_index("tower")
    plane = lax.axis_index("loss") * pipes + lax.axis_index("pipe")

    def tower_at(k):
        return {"tower": partner(tower, k, towers)[0]}

    def plane_at(k):
        q = partner(plane, k, planes)[0]
        return {"loss": q // pipes, "pipe": lax.rem(q, pipes)}

    def block(i):
        at = i * rows
        return pl.multiple_of(at, 8) if rows % 8 == 0 else at

    loads = []
    for n, (src, dst) in enumerate((
        (feats_hbm.at[0, 0], feats),
        (wi_hbm, wi),
        (lens_hbm.at[0], lens),
        (words_hbm.at[0, 0], words),
        (wt_hbm, wt),
        (scale_hbm, scale_ref),
        (shift_hbm, shift_ref),
    )):
        loads.append(pltpu.make_async_copy(src, dst, load_sem.at[n]))
        loads[-1].start()

    barrier = pltpu.get_barrier_semaphore()
    each(1, towers, lambda k: pl.semaphore_signal(
        barrier, inc=1, device_id=tower_at(k), device_id_type=MESH))
    each(1, planes, lambda k: pl.semaphore_signal(
        barrier, inc=1, device_id=plane_at(k), device_id_type=MESH))

    def spread(ref, start, x):
        for c in range(chunks):
            ref[pl.ds(start + c, x.shape[0], stride=chunks), :] = x[:, c * LANES:(c + 1) * LANES]

    def gather(ref, start, n):
        return jnp.concatenate(
            [ref[pl.ds(start + c, n, stride=chunks), :] for c in range(chunks)], axis=1)

    def up(power):
        return jnp.exp(power * -LN2) * STEPS

    def down(power):
        return jnp.exp(power * LN2) * (1.0 / STEPS)

    def encode(raw, flat, power_ref, part):
        most = jnp.max(jnp.abs(raw), axis=1, keepdims=True)
        power = jnp.floor(jnp.log(jnp.maximum(most, 1e-30)) * (1.0 / LN2)) + 1.0
        spread(flat, 0, raw * up(power))
        power_ref[0:group, :] = jnp.broadcast_to(power, (group, LANES))
        for d in range(towers):
            values = jnp.round(flat[d * rows:(d + 1) * rows, :])
            part[d, 0:rows, :] = values.astype(jnp.int32).astype(CODE)
            part[d, span:span + sub, :] = power_ref[
                d * sub:(d + 1) * sub, :].astype(jnp.int32).astype(CODE)

    def scatter(k, part, got, send, recv):
        return pltpu.make_async_remote_copy(
            src_ref=part.at[partner(tower, k, towers)[0]], dst_ref=got.at[k - 1],
            send_sem=send.at[k - 1], recv_sem=recv.at[k - 1],
            device_id=tower_at(k), device_id_type=MESH)

    loads[0].wait()
    loads[1].wait()
    encode(jnp.dot(feats[...], wi[...], preferred_element_type=F32), flat_i, power_i, part_i)
    pl.semaphore_wait(barrier, towers + planes - 2)
    each(1, towers, lambda k: scatter(k, part_i, got_i, s2, r2).start())

    loads[2].wait()
    diagonal = (lax.broadcasted_iota(jnp.int32, (group, group), 0)
                == lax.broadcasted_iota(jnp.int32, (group, group), 1))
    counts = jnp.sum(jnp.where(diagonal, lens[...].astype(F32), 0.0), axis=1, keepdims=True)
    spot = lax.broadcasted_iota(jnp.int32, (group, group * length), 1)
    first = lax.broadcasted_iota(jnp.int32, (group, group * length), 0) * length
    keep = (spot >= first) & (spot < first + counts.astype(jnp.int32))
    keep = jnp.where(keep, 1.0, 0.0).astype(BF16)
    loads[3].wait()
    summed = jnp.dot(keep, words[...].reshape(group * length, words.shape[2]),
                     preferred_element_type=F32)
    pooled = (summed / counts).astype(BF16)
    loads[4].wait()
    encode(jnp.dot(pooled, wt[...], preferred_element_type=F32), flat_t, power_t, part_t)
    each(1, towers, lambda k: scatter(k, part_t, got_t, s1, r1).start())

    def unit(flat, power_ref, part, got, send, recv):
        raw = gather(flat, block(tower), sub) * down(power_ref[pl.ds(tower * sub, sub), 0:1])
        for k in reversed(range(1, towers)):
            scatter(k, part, got, send, recv).wait_recv()
            code[...] = got[k - 1, 0:rows, :].astype(jnp.int32).astype(F32)
            power = got[k - 1, span:span + sub, :].astype(jnp.int32).astype(F32)[:, 0:1]
            raw = raw + gather(code, 0, sub) * down(power)
        size = jnp.sum(raw * raw, axis=-1, keepdims=True) + 1e-06
        return raw * lax.rsqrt(size)

    def give_t(k):
        return pltpu.make_async_remote_copy(
            src_ref=texts.at[plane], dst_ref=texts.at[plane],
            send_sem=s3.at[k - 1], recv_sem=r3.at[k - 1],
            device_id=plane_at(k), device_id_type=MESH)

    def give_i(k):
        return pltpu.make_async_remote_copy(
            src_ref=images.at[tower], dst_ref=images.at[tower],
            send_sem=s4.at[k - 1], recv_sem=r4.at[k - 1],
            device_id=tower_at(k), device_id_type=MESH)

    spread(full_i, block(tower), unit(flat_i, power_i, part_i, got_i, s2, r2))
    images[tower, 0:rows, :] = full_i[pl.ds(block(tower), rows), :].astype(BF16)
    each(1, towers, lambda k: give_i(k).start())
    spread(full_t, block(plane), unit(flat_t, power_t, part_t, got_t, s1, r1))
    texts[plane, 0:rows, :] = full_t[pl.ds(block(plane), rows), :].astype(BF16)
    each(1, planes, lambda k: give_t(k).start())

    def take_i(k):
        give_i(k).wait_recv()
        q = partner(tower, k, towers)[1]
        full_i[pl.ds(block(q), rows), :] = images[q, 0:rows, :].astype(F32)

    def take_t(k):
        give_t(k).wait_recv()
        q = partner(plane, k, planes)[1]
        full_t[pl.ds(block(q), rows), :] = texts[q, 0:rows, :].astype(F32)

    loads[5].wait()
    loads[6].wait()
    scale = scale_ref[0]
    shift = shift_ref[0]
    cols = planes * sub
    each(1, towers, take_i)
    all_i = gather(full_i, 0, group).astype(BF16)
    each(1, planes, take_t)
    all_t = gather(full_t, 0, cols).astype(BF16)
    scores = lax.dot_general(all_i, all_t, (((1,), (1,)), ((), ())), preferred_element_type=F32)
    at_i = lax.broadcasted_iota(jnp.int32, (group, cols), 0) - tower * sub
    at_t = lax.broadcasted_iota(jnp.int32, (group, cols), 1) - plane * sub
    match = jnp.where((at_i == at_t) & (at_i >= 0) & (at_i < sub), 1.0, 0.0)
    grads = jax.nn.sigmoid(scale * scores + shift) - match

    def back_image(k):
        return pltpu.make_async_remote_copy(
            src_ref=term_i.at[partner(tower, k, towers)[0]], dst_ref=back_i.at[k - 1],
            send_sem=s5.at[k - 1], recv_sem=r5.at[k - 1],
            device_id=tower_at(k), device_id_type=MESH)

    def back_text(k):
        return pltpu.make_async_remote_copy(
            src_ref=term_t.at[partner(plane, k, planes)[0]], dst_ref=back_t.at[k - 1],
            send_sem=s6.at[k - 1], recv_sem=r6.at[k - 1],
            device_id=plane_at(k), device_id_type=MESH)

    def stage(n, sums, term):
        for d in range(n):
            term[d, 0:rows, :] = sums[d * rows:(d + 1) * rows, :].astype(WIRE)

    spread(sums_i, 0, jnp.dot(grads.astype(BF16), all_t, preferred_element_type=F32))
    stage(towers, sums_i, term_i)
    each(1, towers, lambda k: back_image(k).start())
    spread(sums_t, 0, jnp.dot(grads.T.astype(BF16), all_i, preferred_element_type=F32))
    stage(planes, sums_t, term_t)
    each(1, planes, lambda k: back_text(k).start())

    def total(sums, me, back, wait, n, out):
        each(1, n, wait)
        value = sums[pl.ds(block(me), rows), :]
        value = scale * (value + jnp.sum(back[:, 0:rows, :].astype(F32), axis=0))
        code[...] = value
        out[:, 0, :] = gather(code, 0, sub)

    total(sums_t, plane, back_t, lambda k: back_text(k).wait_recv(), planes, text_out)
    total(sums_i, tower, back_i, lambda k: back_image(k).wait_recv(), towers, image_out)

    each(1, towers, lambda k: scatter(k, part_t, got_t, s1, r1).wait_send())
    each(1, towers, lambda k: scatter(k, part_i, got_i, s2, r2).wait_send())
    each(1, planes, lambda k: give_t(k).wait_send())
    each(1, towers, lambda k: give_i(k).wait_send())
    each(1, towers, lambda k: back_image(k).wait_send())
    each(1, planes, lambda k: back_text(k).wait_send())


def finish(image_ref, text_ref, image_out, text_out):
    image_out[...] = image_ref[...]
    text_out[...] = text_ref[...]


def up_to(n, m):
    return -(-n // m) * m


def per_device(towers, pipes, planes, image_feats, text_tokens, lengths, w_image, w_text,
               logit_scale, logit_bias):
    group = image_feats.shape[2]
    emb = w_image.shape[1]
    sub = group // towers
    rows = sub * emb // LANES
    span = up_to(rows, 8)
    note = up_to(span + sub, 16)
    out = jax.ShapeDtypeStruct((sub, 1, emb), F32)
    sems = []
    for n in (towers, towers, planes, towers, towers, planes):
        sems += [pltpu.SemaphoreType.DMA((n - 1,))] * 2
    outs = pl.pallas_call(
        functools.partial(kernel, sub, towers, pipes, planes),
        out_shape=(out, out),
        in_specs=[pl.BlockSpec(memory_space=pl.ANY)] * 7,
        out_specs=(pl.BlockSpec(memory_space=pltpu.VMEM),) * 2,
        scratch_shapes=[
            pltpu.SMEM(logit_scale.shape, F32),
            pltpu.SMEM(logit_bias.shape, F32),
            pltpu.VMEM(image_feats.shape[2:], image_feats.dtype),
            pltpu.VMEM(text_tokens.shape[2:], text_tokens.dtype),
            pltpu.VMEM(lengths.shape[1:], lengths.dtype),
            pltpu.VMEM(w_image.shape, w_image.dtype),
            pltpu.VMEM(w_text.shape, w_text.dtype),
            pltpu.VMEM((towers * rows, LANES), F32),
            pltpu.VMEM((towers * rows, LANES), F32),
            pltpu.VMEM((up_to(group, 8), LANES), F32),
            pltpu.VMEM((up_to(group, 8), LANES), F32),
            pltpu.VMEM((towers, note, LANES), CODE),
            pltpu.VMEM((towers, note, LANES), CODE),
            pltpu.VMEM((towers - 1, note, LANES), CODE),
            pltpu.VMEM((towers - 1, note, LANES), CODE),
            pltpu.VMEM((rows, LANES), F32),
            pltpu.VMEM((towers * rows, LANES), F32),
            pltpu.VMEM((planes * rows, LANES), F32),
            pltpu.VMEM((towers, span, LANES), BF16),
            pltpu.VMEM((planes, span, LANES), BF16),
            pltpu.VMEM((towers * rows, LANES), F32),
            pltpu.VMEM((planes * rows, LANES), F32),
            pltpu.VMEM((towers, span, LANES), WIRE),
            pltpu.VMEM((planes, span, LANES), WIRE),
            pltpu.VMEM((towers - 1, span, LANES), WIRE),
            pltpu.VMEM((planes - 1, span, LANES), WIRE),
            pltpu.SemaphoreType.DMA((7,)),
        ] + sems,
        compiler_params=pltpu.CompilerParams(collective_id=0, has_side_effects=True),
    )(logit_scale, logit_bias, image_feats, text_tokens, lengths, w_image, w_text)
    outs = pl.pallas_call(
        finish,
        out_shape=(out, out),
        in_specs=[pl.BlockSpec(memory_space=pltpu.VMEM)] * 2,
        out_specs=(pl.BlockSpec(memory_space=pltpu.VMEM),) * 2,
    )(*outs)
    return tuple(o.reshape(1, 1, sub, emb) for o in outs)


def solution(mesh):
    shape = dict(mesh.shape)
    planes = shape["loss"] * shape["pipe"]
    return jax.shard_map(
        functools.partial(per_device, shape["tower"], shape["pipe"], planes),
        mesh=mesh,
        in_specs=(
            P("loss", "pipe", None, "tower"),
            P("loss", "pipe", None, None, "tower"),
            P("loss", "pipe", None),
            P("tower", None),
            P("tower", None),
            P(),
            P(),
        ),
        out_specs=(P("loss", "pipe", "tower", None), P("loss", "pipe", "tower", None)),
        check_vma=False,
    )
```

time: 26.9 us -> 25 us (0.929)
  Pallas kernels: 24.7 us -> 22.8 us
    pallas_call x1, Pallas kernels: 23.3 us -> 21.4 us  [per_device(): pl.pallas_call(functools.partial(kernel, sub, towers, pipes, planes), out...]
where the time goes in v1:
time: 25 us; the launch traced here: 24.8 us
  Pallas kernels  22.8 us (91%)
  between operations  1.93 us (8%)
    pallas_call x1, Pallas kernels, per_device(): pl.pallas_call(functools.partial(kernel, sub, towers, pipes, planes), out...  21.4 us
    pallas_call x1, Pallas kernels, per_device(): pl.pallas_call(finish, out_shape=(out, out), in_specs=[pl.BlockSpec(memor...  1.42 us

profile of v1, /device:TPU:0, one launch (start us, length us, event | category | flops | bytes accessed | tf_op | source)
XLA Modules:
  0.0 24.8 jit_solution(5827091674083978789)
XLA Ops:
  1.9 21.4 %shard_map.86 = (f32[6,1,1536]{2,1,0:T(1,128)}, f32[6,1,1536]{2,1,0:T(1,128)}) custom-call(f32[1]{0:T(128)S(6)} %copy.11.scale_hbm, f32[1]{0:T(128)S(6)} %copy.12.shift_hbm, bf16[1,1,24,384]{3,2,1,0:T(8,128)(2,1)} %feats_hbm.1, bf16[1,1,24,64,288]{4,3,2,1,0:T(8,128)(2,1)} %words_hbm.1, s32[1,1,24]{2,1,0:T(1,128)} %lens_hbm.1, bf16[384,1536]{1,0:T(8,128)(2,1)} %wi_hbm.1, ...), custom_call_target="tpu_custom_call" | custom-call | tf_op jit(solution)/shard_map/pallas_call | solution.py:256
  23.3 1.4 %shard_map.87 = (f32[6,1,1536]{2,1,0:T(1,128)}, f32[6,1,1536]{2,1,0:T(1,128)}) custom-call(f32[6,1,1536]{2,1,0:T(1,128)} %get-tuple-element.6.image_ref, f32[6,1,1536]{2,1,0:T(1,128)} %get-tuple-element.7.text_ref), custom_call_target="tpu_custom_call" | custom-call | tf_op jit(solution)/shard_map/pallas_call | solution.py:292

commit v2 on v1

--- a/solution.py
+++ b/solution.py
@@ -253,6 +253,8 @@
     sems = []
     for n in (towers, towers, planes, towers, towers, planes):
         sems += [pltpu.SemaphoreType.DMA((n - 1,))] * 2
+    arrays = [pltpu.with_memory_space_constraint(x, pltpu.HBM) for x in (
+        image_feats, text_tokens, lengths, w_image, w_text)]
     outs = pl.pallas_call(
         functools.partial(kernel, sub, towers, pipes, planes),
         out_shape=(out, out),
@@ -287,13 +289,15 @@
             pltpu.VMEM((planes - 1, span, LANES), WIRE),
             pltpu.SemaphoreType.DMA((7,)),
         ] + sems,
-        compiler_params=pltpu.CompilerParams(collective_id=0, has_side_effects=True),
-    )(logit_scale, logit_bias, image_feats, text_tokens, lengths, w_image, w_text)
+        compiler_params=pltpu.CompilerParams(
+            collective_id=0, has_side_effects=True, vmem_limit_bytes=24 * 2**20),
+    )(logit_scale, logit_bias, *arrays)
     outs = pl.pallas_call(
         finish,
         out_shape=(out, out),
         in_specs=[pl.BlockSpec(memory_space=pltpu.VMEM)] * 2,
         out_specs=(pl.BlockSpec(memory_space=pltpu.VMEM),) * 2,
+        compiler_params=pltpu.CompilerParams(vmem_limit_bytes=2**20),
     )(*outs)
     return tuple(o.reshape(1, 1, sub, emb) for o in outs)
 

time: 25 us -> 23.5 us (0.940)
  Pallas kernels: 22.8 us -> 21.4 us
    pallas_call x1, Pallas kernels: 1.42 us -> 0.64 us  [per_device(): pl.pallas_call(finish, out_shape=(out, out), in_specs=[pl.BlockSpec(memor...]
    pallas_call x1, Pallas kernels: 21.4 us -> 20.8 us  [per_device(): pl.pallas_call(functools.partial(kernel, sub, towers, pipes, planes), out...]
where the time goes in v2:
time: 23.5 us; the launch traced here: 23.4 us
  Pallas kernels  21.4 us (91%)
  between operations  1.93 us (8%)
    pallas_call x1, Pallas kernels, per_device(): pl.pallas_call(functools.partial(kernel, sub, towers, pipes, planes), out...  20.8 us
    pallas_call x1, Pallas kernels, per_device(): pl.pallas_call(finish, out_shape=(out, out), in_specs=[pl.BlockSpec(memor...  0.64 us

profile of v2, /device:TPU:0, one launch (start us, length us, event | category | flops | bytes accessed | tf_op | source)
XLA Modules:
  0.0 23.4 jit_solution(2403972219944139813)
XLA Ops:
  1.9 20.8 %shard_map.86 = (f32[6,1,1536]{2,1,0:T(1,128)S(1)}, f32[6,1,1536]{2,1,0:T(1,128)S(1)}) custom-call(f32[1]{0:T(128)S(6)} %copy.11.scale_hbm, f32[1]{0:T(128)S(6)} %copy.12.shift_hbm, bf16[1,1,24,384]{3,2,1,0:T(8,128)(2,1)} %feats_hbm.1, bf16[1,1,24,64,288]{4,3,2,1,0:T(8,128)(2,1)} %words_hbm.1, s32[1,1,24]{2,1,0:T(1,128)} %lens_hbm.1, ...), custom_call_target="tpu_custom_call" | custom-call | tf_op jit(solution)/shard_map/pallas_call | solution.py:258
  22.7 0.6 %shard_map.87 = (f32[6,1,1536]{2,1,0:T(1,128)}, f32[6,1,1536]{2,1,0:T(1,128)}) custom-call(f32[6,1,1536]{2,1,0:T(1,128)S(1)} %get-tuple-element.6.image_ref, f32[6,1,1536]{2,1,0:T(1,128)S(1)} %get-tuple-element.7.text_ref), custom_call_target="tpu_custom_call" | custom-call | tf_op jit(solution)/shard_map/pallas_call | solution.py:295

commit v3 on v2

--- a/solution.py
+++ b/solution.py
@@ -24,6 +24,14 @@
             body(k)
     else:
         lax.fori_loop(lo, hi, lambda k, c: (body(k), c)[1], 0)
+
+
+def near(lo, hi, body):
+    if hi - lo <= UNROLL:
+        for k in sorted(range(lo, hi), key=lambda k: (bin(k).count("1"), k)):
+            body(k)
+    else:
+        each(lo, hi, body)
 
 
 def partner(me, k, n):
@@ -67,11 +75,11 @@
 
     loads = []
     for n, (src, dst) in enumerate((
-        (feats_hbm.at[0, 0], feats),
-        (wi_hbm, wi),
         (lens_hbm.at[0], lens),
         (words_hbm.at[0, 0], words),
         (wt_hbm, wt),
+        (feats_hbm.at[0, 0], feats),
+        (wi_hbm, wi),
         (scale_hbm, scale_ref),
         (shift_hbm, shift_ref),
     )):
@@ -116,12 +124,6 @@
             device_id=tower_at(k), device_id_type=MESH)
 
     loads[0].wait()
-    loads[1].wait()
-    encode(jnp.dot(feats[...], wi[...], preferred_element_type=F32), flat_i, power_i, part_i)
-    pl.semaphore_wait(barrier, towers + planes - 2)
-    each(1, towers, lambda k: scatter(k, part_i, got_i, s2, r2).start())
-
-    loads[2].wait()
     diagonal = (lax.broadcasted_iota(jnp.int32, (group, group), 0)
                 == lax.broadcasted_iota(jnp.int32, (group, group), 1))
     counts = jnp.sum(jnp.where(diagonal, lens[...].astype(F32), 0.0), axis=1, keepdims=True)
@@ -129,13 +131,19 @@
     first = lax.broadcasted_iota(jnp.int32, (group, group * length), 0) * length
     keep = (spot >= first) & (spot < first + counts.astype(jnp.int32))
     keep = jnp.where(keep, 1.0, 0.0).astype(BF16)
-    loads[3].wait()
+    loads[1].wait()
     summed = jnp.dot(keep, words[...].reshape(group * length, words.shape[2]),
                      preferred_element_type=F32)
     pooled = (summed / counts).astype(BF16)
+    loads[2].wait()
+    encode(jnp.dot(pooled, wt[...], preferred_element_type=F32), flat_t, power_t, part_t)
+    pl.semaphore_wait(barrier, towers + planes - 2)
+    each(1, towers, lambda k: scatter(k, part_t, got_t, s1, r1).start())
+
+    loads[3].wait()
     loads[4].wait()
-    encode(jnp.dot(pooled, wt[...], preferred_element_type=F32), flat_t, power_t, part_t)
-    each(1, towers, lambda k: scatter(k, part_t, got_t, s1, r1).start())
+    encode(jnp.dot(feats[...], wi[...], preferred_element_type=F32), flat_i, power_i, part_i)
+    each(1, towers, lambda k: scatter(k, part_i, got_i, s2, r2).start())
 
     def unit(flat, power_ref, part, got, send, recv):
         raw = gather(flat, block(tower), sub) * down(power_ref[pl.ds(tower * sub, sub), 0:1])
@@ -159,12 +167,12 @@
             send_sem=s4.at[k - 1], recv_sem=r4.at[k - 1],
             device_id=tower_at(k), device_id_type=MESH)
 
+    spread(full_t, block(plane), unit(flat_t, power_t, part_t, got_t, s1, r1))
+    texts[plane, 0:rows, :] = full_t[pl.ds(block(plane), rows), :].astype(BF16)
+    each(1, planes, lambda k: give_t(k).start())
     spread(full_i, block(tower), unit(flat_i, power_i, part_i, got_i, s2, r2))
     images[tower, 0:rows, :] = full_i[pl.ds(block(tower), rows), :].astype(BF16)
     each(1, towers, lambda k: give_i(k).start())
-    spread(full_t, block(plane), unit(flat_t, power_t, part_t, got_t, s1, r1))
-    texts[plane, 0:rows, :] = full_t[pl.ds(block(plane), rows), :].astype(BF16)
-    each(1, planes, lambda k: give_t(k).start())
 
     def take_i(k):
         give_i(k).wait_recv()
@@ -181,9 +189,9 @@
     scale = scale_ref[0]
     shift = shift_ref[0]
     cols = planes * sub
-    each(1, towers, take_i)
+    near(1, towers, take_i)
     all_i = gather(full_i, 0, group).astype(BF16)
-    each(1, planes, take_t)
+    near(1, planes, take_t)
     all_t = gather(full_t, 0, cols).astype(BF16)
     scores = lax.dot_general(all_i, all_t, (((1,), (1,)), ((), ())), preferred_element_type=F32)
     at_i = lax.broadcasted_iota(jnp.int32, (group, cols), 0) - tower * sub
@@ -215,7 +223,7 @@
     each(1, planes, lambda k: back_text(k).start())
 
     def total(sums, me, back, wait, n, out):
-        each(1, n, wait)
+        near(1, n, wait)
         value = sums[pl.ds(block(me), rows), :]
         value = scale * (value + jnp.sum(back[:, 0:rows, :].astype(F32), axis=0))
         code[...] = value

time: 23.5 us -> 22.5 us (0.957)
  Pallas kernels: 21.4 us -> 20.4 us
    pallas_call x1, Pallas kernels: 20.8 us -> 19.7 us  [per_device(): pl.pallas_call(functools.partial(kernel, sub, towers, pipes, planes), out...]
where the time goes in v3:
time: 22.5 us; the launch traced here: 22.3 us
  Pallas kernels  20.4 us (91%)
  between operations  1.93 us (9%)
    pallas_call x1, Pallas kernels, per_device(): pl.pallas_call(functools.partial(kernel, sub, towers, pipes, planes), out...  19.7 us
    pallas_call x1, Pallas kernels, per_device(): pl.pallas_call(finish, out_shape=(out, out), in_specs=[pl.BlockSpec(memor...  0.64 us

profile of v3, /device:TPU:0, one launch (start us, length us, event | category | flops | bytes accessed | tf_op | source)
XLA Modules:
  0.0 22.3 jit_solution(12871174933647777813)
XLA Ops:
  1.9 19.7 %shard_map.86 = (f32[6,1,1536]{2,1,0:T(1,128)S(1)}, f32[6,1,1536]{2,1,0:T(1,128)S(1)}) custom-call(f32[1]{0:T(128)S(6)} %copy.11.scale_hbm, f32[1]{0:T(128)S(6)} %copy.12.shift_hbm, bf16[1,1,24,384]{3,2,1,0:T(8,128)(2,1)} %feats_hbm.1, bf16[1,1,24,64,288]{4,3,2,1,0:T(8,128)(2,1)} %words_hbm.1, s32[1,1,24]{2,1,0:T(1,128)} %lens_hbm.1, ...), custom_call_target="tpu_custom_call" | custom-call | tf_op jit(solution)/shard_map/pallas_call | solution.py:266
  21.7 0.6 %shard_map.87 = (f32[6,1,1536]{2,1,0:T(1,128)}, f32[6,1,1536]{2,1,0:T(1,128)}) custom-call(f32[6,1,1536]{2,1,0:T(1,128)S(1)} %get-tuple-element.6.image_ref, f32[6,1,1536]{2,1,0:T(1,128)S(1)} %get-tuple-element.7.text_ref), custom_call_target="tpu_custom_call" | custom-call | tf_op jit(solution)/shard_map/pallas_call | solution.py:303

commit v4 on v3

--- a/solution.py
+++ b/solution.py
@@ -15,7 +15,6 @@
 UNROLL = 16
 LANES = 128
 STEPS = 32752.0
-LN2 = 0.6931471805599453
 
 
 def each(lo, hi, body):
@@ -49,9 +48,10 @@
     scale_hbm, shift_hbm, feats_hbm, words_hbm, lens_hbm, wi_hbm, wt_hbm,
     image_out, text_out,
     scale_ref, shift_ref, feats, words, lens, wi, wt,
-    flat_i, flat_t, power_i, power_t, part_i, part_t, got_i, got_t, code,
+    flat_i, flat_t, down_i, down_t, note_i, note_t, told_i, told_t,
+    part_i, part_t, got_i, got_t, code,
     full_i, full_t, images, texts, sums_i, sums_t, term_i, term_t, back_i, back_t,
-    load_sem, s1, r1, s2, r2, s3, r3, s4, r4, s5, r5, s6, r6,
+    load_sem, s1, r1, s2, r2, s3, r3, s4, r4, s5, r5, s6, r6, s7, r7, s8, r8,
 ):
     group, width = feats.shape
     length = words.shape[1]
@@ -73,18 +73,19 @@
         at = i * rows
         return pl.multiple_of(at, 8) if rows % 8 == 0 else at
 
+    batch = 8 if group % 8 == 0 else group
+    parts = group // batch
     loads = []
-    for n, (src, dst) in enumerate((
-        (lens_hbm.at[0], lens),
-        (words_hbm.at[0, 0], words),
-        (wt_hbm, wt),
-        (feats_hbm.at[0, 0], feats),
-        (wi_hbm, wi),
-        (scale_hbm, scale_ref),
-        (shift_hbm, shift_ref),
-    )):
+    for n, (src, dst) in enumerate(
+        [(lens_hbm.at[0], lens)]
+        + [(words_hbm.at[0, 0, c * batch:(c + 1) * batch], words.at[c * batch:(c + 1) * batch])
+           for c in range(parts)]
+        + [(wt_hbm, wt), (feats_hbm.at[0, 0], feats), (wi_hbm, wi),
+           (scale_hbm, scale_ref), (shift_hbm, shift_ref)]
+    ):
         loads.append(pltpu.make_async_copy(src, dst, load_sem.at[n]))
         loads[-1].start()
+    load_lens, *load_words, load_wt, load_feats, load_wi, load_scale, load_shift = loads
 
     barrier = pltpu.get_barrier_semaphore()
     each(1, towers, lambda k: pl.semaphore_signal(
@@ -100,22 +101,19 @@
         return jnp.concatenate(
             [ref[pl.ds(start + c, n, stride=chunks), :] for c in range(chunks)], axis=1)
 
-    def up(power):
-        return jnp.exp(power * -LN2) * STEPS
-
-    def down(power):
-        return jnp.exp(power * LN2) * (1.0 / STEPS)
-
-    def encode(raw, flat, power_ref, part):
-        most = jnp.max(jnp.abs(raw), axis=1, keepdims=True)
-        power = jnp.floor(jnp.log(jnp.maximum(most, 1e-30)) * (1.0 / LN2)) + 1.0
-        spread(flat, 0, raw * up(power))
-        power_ref[0:group, :] = jnp.broadcast_to(power, (group, LANES))
+    def encode(raw, flat, down, part, note):
+        most = jnp.maximum(jnp.max(jnp.abs(raw), axis=1, keepdims=True), 1e-30)
+        spread(flat, 0, raw * (STEPS / most))
+        step = most * (1.0 / STEPS)
+        down[0:group, :] = jnp.broadcast_to(step, (group, LANES))
+        row = lax.broadcasted_iota(jnp.int32, (group, LANES), 0)
+        lane = lax.broadcasted_iota(jnp.int32, (group, LANES), 1)
+        for d in range(towers):
+            mine = (row == lane + d * sub) & (lane < sub)
+            note[d] = jnp.sum(jnp.where(mine, step, 0.0), axis=0, keepdims=True)
         for d in range(towers):
             values = jnp.round(flat[d * rows:(d + 1) * rows, :])
             part[d, 0:rows, :] = values.astype(jnp.int32).astype(CODE)
-            part[d, span:span + sub, :] = power_ref[
-                d * sub:(d + 1) * sub, :].astype(jnp.int32).astype(CODE)
 
     def scatter(k, part, got, send, recv):
         return pltpu.make_async_remote_copy(
@@ -123,35 +121,45 @@
             send_sem=send.at[k - 1], recv_sem=recv.at[k - 1],
             device_id=tower_at(k), device_id_type=MESH)
 
-    loads[0].wait()
-    diagonal = (lax.broadcasted_iota(jnp.int32, (group, group), 0)
-                == lax.broadcasted_iota(jnp.int32, (group, group), 1))
-    counts = jnp.sum(jnp.where(diagonal, lens[...].astype(F32), 0.0), axis=1, keepdims=True)
-    spot = lax.broadcasted_iota(jnp.int32, (group, group * length), 1)
-    first = lax.broadcasted_iota(jnp.int32, (group, group * length), 0) * length
-    keep = (spot >= first) & (spot < first + counts.astype(jnp.int32))
-    keep = jnp.where(keep, 1.0, 0.0).astype(BF16)
-    loads[1].wait()
-    summed = jnp.dot(keep, words[...].reshape(group * length, words.shape[2]),
-                     preferred_element_type=F32)
-    pooled = (summed / counts).astype(BF16)
-    loads[2].wait()
-    encode(jnp.dot(pooled, wt[...], preferred_element_type=F32), flat_t, power_t, part_t)
+    load_lens.wait()
+    counts = lens[...].astype(F32)
+    pooled = []
+    for c in range(parts):
+        row = lax.broadcasted_iota(jnp.int32, (batch, group), 0) + c * batch
+        mine = row == lax.broadcasted_iota(jnp.int32, (batch, group), 1)
+        count = jnp.sum(jnp.where(mine, counts, 0.0), axis=1, keepdims=True)
+        spot = lax.broadcasted_iota(jnp.int32, (batch, batch * length), 1)
+        first = lax.broadcasted_iota(jnp.int32, (batch, batch * length), 0) * length
+        keep = (spot >= first) & (spot < first + count.astype(jnp.int32))
+        keep = jnp.where(keep, 1.0, 0.0).astype(BF16)
+        load_words[c].wait()
+        summed = jnp.dot(
+            keep, words[c * batch:(c + 1) * batch].reshape(batch * length, words.shape[2]),
+            preferred_element_type=F32)
+        pooled.append(summed / count)
+    pooled = jnp.concatenate(pooled, axis=0).astype(BF16)
+    load_wt.wait()
+    encode(jnp.dot(pooled, wt[...], preferred_element_type=F32), flat_t, down_t, part_t, note_t)
     pl.semaphore_wait(barrier, towers + planes - 2)
+    each(1, towers, lambda k: scatter(k, note_t, told_t, s7, r7).start())
     each(1, towers, lambda k: scatter(k, part_t, got_t, s1, r1).start())
 
-    loads[3].wait()
-    loads[4].wait()
-    encode(jnp.dot(feats[...], wi[...], preferred_element_type=F32), flat_i, power_i, part_i)
+    load_feats.wait()
+    load_wi.wait()
+    encode(jnp.dot(feats[...], wi[...], preferred_element_type=F32), flat_i, down_i, part_i, note_i)
+    each(1, towers, lambda k: scatter(k, note_i, told_i, s8, r8).start())
     each(1, towers, lambda k: scatter(k, part_i, got_i, s2, r2).start())
 
-    def unit(flat, power_ref, part, got, send, recv):
-        raw = gather(flat, block(tower), sub) * down(power_ref[pl.ds(tower * sub, sub), 0:1])
+    def unit(flat, down, part, got, send, recv, note, told, note_send, note_recv):
+        raw = gather(flat, block(tower), sub) * down[pl.ds(tower * sub, sub), 0:1]
+        mine = (lax.broadcasted_iota(jnp.int32, (sub, LANES), 0)
+                == lax.broadcasted_iota(jnp.int32, (sub, LANES), 1))
         for k in reversed(range(1, towers)):
+            scatter(k, note, told, note_send, note_recv).wait_recv()
+            step = jnp.sum(jnp.where(mine, told[k - 1], 0.0), axis=1, keepdims=True)
             scatter(k, part, got, send, recv).wait_recv()
             code[...] = got[k - 1, 0:rows, :].astype(jnp.int32).astype(F32)
-            power = got[k - 1, span:span + sub, :].astype(jnp.int32).astype(F32)[:, 0:1]
-            raw = raw + gather(code, 0, sub) * down(power)
+            raw = raw + gather(code, 0, sub) * step
         size = jnp.sum(raw * raw, axis=-1, keepdims=True) + 1e-06
         return raw * lax.rsqrt(size)
 
@@ -167,10 +175,12 @@
             send_sem=s4.at[k - 1], recv_sem=r4.at[k - 1],
             device_id=tower_at(k), device_id_type=MESH)
 
-    spread(full_t, block(plane), unit(flat_t, power_t, part_t, got_t, s1, r1))
+    spread(full_t, block(plane), unit(
+        flat_t, down_t, part_t, got_t, s1, r1, note_t, told_t, s7, r7))
     texts[plane, 0:rows, :] = full_t[pl.ds(block(plane), rows), :].astype(BF16)
     each(1, planes, lambda k: give_t(k).start())
-    spread(full_i, block(tower), unit(flat_i, power_i, part_i, got_i, s2, r2))
+    spread(full_i, block(tower), unit(
+        flat_i, down_i, part_i, got_i, s2, r2, note_i, told_i, s8, r8))
     images[tower, 0:rows, :] = full_i[pl.ds(block(tower), rows), :].astype(BF16)
     each(1, towers, lambda k: give_i(k).start())
 
@@ -184,15 +194,15 @@
         q = partner(plane, k, planes)[1]
         full_t[pl.ds(block(q), rows), :] = texts[q, 0:rows, :].astype(F32)
 
-    loads[5].wait()
-    loads[6].wait()
+    load_scale.wait()
+    load_shift.wait()
     scale = scale_ref[0]
     shift = shift_ref[0]
     cols = planes * sub
+    near(1, planes, take_t)
+    all_t = gather(full_t, 0, cols).astype(BF16)
     near(1, towers, take_i)
     all_i = gather(full_i, 0, group).astype(BF16)
-    near(1, planes, take_t)
-    all_t = gather(full_t, 0, cols).astype(BF16)
     scores = lax.dot_general(all_i, all_t, (((1,), (1,)), ((), ())), preferred_element_type=F32)
     at_i = lax.broadcasted_iota(jnp.int32, (group, cols), 0) - tower * sub
     at_t = lax.broadcasted_iota(jnp.int32, (group, cols), 1) - plane * sub
@@ -232,6 +242,8 @@
     total(sums_t, plane, back_t, lambda k: back_text(k).wait_recv(), planes, text_out)
     total(sums_i, tower, back_i, lambda k: back_image(k).wait_recv(), towers, image_out)
 
+    each(1, towers, lambda k: scatter(k, note_t, told_t, s7, r7).wait_send())
+    each(1, towers, lambda k: scatter(k, note_i, told_i, s8, r8).wait_send())
     each(1, towers, lambda k: scatter(k, part_t, got_t, s1, r1).wait_send())
     each(1, towers, lambda k: scatter(k, part_i, got_i, s2, r2).wait_send())
     each(1, planes, lambda k: give_t(k).wait_send())
@@ -256,10 +268,9 @@
     sub = group // towers
     rows = sub * emb // LANES
     span = up_to(rows, 8)
-    note = up_to(span + sub, 16)
     out = jax.ShapeDtypeStruct((sub, 1, emb), F32)
     sems = []
-    for n in (towers, towers, planes, towers, towers, planes):
+    for n in (towers, towers, planes, towers, towers, planes, towers, towers):
         sems += [pltpu.SemaphoreType.DMA((n - 1,))] * 2
     arrays = [pltpu.with_memory_space_constraint(x, pltpu.HBM) for x in (
         image_feats, text_tokens, lengths, w_image, w_text)]
@@ -280,10 +291,14 @@
             pltpu.VMEM((towers * rows, LANES), F32),
             pltpu.VMEM((up_to(group, 8), LANES), F32),
             pltpu.VMEM((up_to(group, 8), LANES), F32),
-            pltpu.VMEM((towers, note, LANES), CODE),
-            pltpu.VMEM((towers, note, LANES), CODE),
-            pltpu.VMEM((towers - 1, note, LANES), CODE),
-            pltpu.VMEM((towers - 1, note, LANES), CODE),
+            pltpu.VMEM((towers, 1, LANES), F32),
+            pltpu.VMEM((towers, 1, LANES), F32),
+            pltpu.VMEM((towers - 1, 1, LANES), F32),
+            pltpu.VMEM((towers - 1, 1, LANES), F32),
+            pltpu.VMEM((towers, span, LANES), CODE),
+            pltpu.VMEM((towers, span, LANES), CODE),
+            pltpu.VMEM((towers - 1, span, LANES), CODE),
+            pltpu.VMEM((towers - 1, span, LANES), CODE),
             pltpu.VMEM((rows, LANES), F32),
             pltpu.VMEM((towers * rows, LANES), F32),
             pltpu.VMEM((planes * rows, LANES), F32),
@@ -295,7 +310,7 @@
             pltpu.VMEM((planes, span, LANES), WIRE),
             pltpu.VMEM((towers - 1, span, LANES), WIRE),
             pltpu.VMEM((planes - 1, span, LANES), WIRE),
-            pltpu.SemaphoreType.DMA((7,)),
+            pltpu.SemaphoreType.DMA((6 + group // (8 if group % 8 == 0 else group),)),
         ] + sems,
         compiler_params=pltpu.CompilerParams(
             collective_id=0, has_side_effects=True, vmem_limit_bytes=24 * 2**20),

time: 22.5 us -> 22.3 us (level)
  no operation moved by 1% of the time
where the time goes in v4:
time: 22.3 us; the launch traced here: 22.1 us
  Pallas kernels  20.2 us (91%)
  between operations  1.93 us (9%)
    pallas_call x1, Pallas kernels, per_device(): pl.pallas_call(functools.partial(kernel, sub, towers, pipes, planes), out...  19.5 us
    pallas_call x1, Pallas kernels, per_device(): pl.pallas_call(finish, out_shape=(out, out), in_specs=[pl.BlockSpec(memor...  0.64 us

profile of v4, /device:TPU:0, one launch (start us, length us, event | category | flops | bytes accessed | tf_op | source)
XLA Modules:
  0.0 22.1 jit_solution(16911233077984368125)
XLA Ops:
  1.9 19.5 %shard_map.86 = (f32[6,1,1536]{2,1,0:T(1,128)S(1)}, f32[6,1,1536]{2,1,0:T(1,128)S(1)}) custom-call(f32[1]{0:T(128)S(6)} %copy.11.scale_hbm, f32[1]{0:T(128)S(6)} %copy.12.shift_hbm, bf16[1,1,24,384]{3,2,1,0:T(8,128)(2,1)} %feats_hbm.1, bf16[1,1,24,64,288]{4,3,2,1,0:T(8,128)(2,1)} %words_hbm.1, s32[1,1,24]{2,1,0:T(1,128)} %lens_hbm.1, ...), custom_call_target="tpu_custom_call" | custom-call | tf_op jit(solution)/shard_map/pallas_call | solution.py:277
  21.5 0.6 %shard_map.87 = (f32[6,1,1536]{2,1,0:T(1,128)}, f32[6,1,1536]{2,1,0:T(1,128)}) custom-call(f32[6,1,1536]{2,1,0:T(1,128)S(1)} %get-tuple-element.6.image_ref, f32[6,1,1536]{2,1,0:T(1,128)S(1)} %get-tuple-element.7.text_ref), custom_call_target="tpu_custom_call" | custom-call | tf_op jit(solution)/shard_map/pallas_call | solution.py:318

commit v5 on v4

--- a/solution.py
+++ b/solution.py
@@ -73,6 +73,9 @@
         at = i * rows
         return pl.multiple_of(at, 8) if rows % 8 == 0 else at
 
+    barrier = pltpu.get_barrier_semaphore()
+    each(1, towers, lambda k: pl.semaphore_signal(
+        barrier, inc=1, device_id=tower_at(k), device_id_type=MESH))
     batch = 8 if group % 8 == 0 else group
     parts = group // batch
     loads = []
@@ -87,9 +90,6 @@
         loads[-1].start()
     load_lens, *load_words, load_wt, load_feats, load_wi, load_scale, load_shift = loads
 
-    barrier = pltpu.get_barrier_semaphore()
-    each(1, towers, lambda k: pl.semaphore_signal(
-        barrier, inc=1, device_id=tower_at(k), device_id_type=MESH))
     each(1, planes, lambda k: pl.semaphore_signal(
         barrier, inc=1, device_id=plane_at(k), device_id_type=MESH))
 
@@ -154,7 +154,7 @@
         raw = gather(flat, block(tower), sub) * down[pl.ds(tower * sub, sub), 0:1]
         mine = (lax.broadcasted_iota(jnp.int32, (sub, LANES), 0)
                 == lax.broadcasted_iota(jnp.int32, (sub, LANES), 1))
-        for k in reversed(range(1, towers)):
+        for k in sorted(range(1, towers), key=lambda k: (bin(k).count("1"), k)):
             scatter(k, note, told, note_send, note_recv).wait_recv()
             step = jnp.sum(jnp.where(mine, told[k - 1], 0.0), axis=1, keepdims=True)
             scatter(k, part, got, send, recv).wait_recv()

time: 22.3 us -> 22.3 us (level)
  no operation moved by 1% of the time
where the time goes in v5:
time: 22.3 us; the launch traced here: 22.1 us
  Pallas kernels  20.2 us (91%)
  between operations  1.93 us (9%)
    pallas_call x1, Pallas kernels, per_device(): pl.pallas_call(functools.partial(kernel, sub, towers, pipes, planes), out...  19.5 us
    pallas_call x1, Pallas kernels, per_device(): pl.pallas_call(finish, out_shape=(out, out), in_specs=[pl.BlockSpec(memor...  0.64 us

profile of v5, /device:TPU:0, one launch (start us, length us, event | category | flops | bytes accessed | tf_op | source)
XLA Modules:
  0.0 22.1 jit_solution(17723998631491562423)
XLA Ops:
  1.9 19.5 %shard_map.86 = (f32[6,1,1536]{2,1,0:T(1,128)S(1)}, f32[6,1,1536]{2,1,0:T(1,128)S(1)}) custom-call(f32[1]{0:T(128)S(6)} %copy.11.scale_hbm, f32[1]{0:T(128)S(6)} %copy.12.shift_hbm, bf16[1,1,24,384]{3,2,1,0:T(8,128)(2,1)} %feats_hbm.1, bf16[1,1,24,64,288]{4,3,2,1,0:T(8,128)(2,1)} %words_hbm.1, s32[1,1,24]{2,1,0:T(1,128)} %lens_hbm.1, ...), custom_call_target="tpu_custom_call" | custom-call | tf_op jit(solution)/shard_map/pallas_call | solution.py:277
  21.5 0.6 %shard_map.87 = (f32[6,1,1536]{2,1,0:T(1,128)}, f32[6,1,1536]{2,1,0:T(1,128)}) custom-call(f32[6,1,1536]{2,1,0:T(1,128)S(1)} %get-tuple-element.6.image_ref, f32[6,1,1536]{2,1,0:T(1,128)S(1)} %get-tuple-element.7.text_ref), custom_call_target="tpu_custom_call" | custom-call | tf_op jit(solution)/shard_map/pallas_call | solution.py:318

commit v6 on v5

--- a/solution.py
+++ b/solution.py
@@ -34,6 +34,8 @@
 
 
 def partner(me, k, n):
+    if isinstance(k, tuple):
+        return k[1], k[1]
     if n <= UNROLL and n & (n - 1) == 0:
         q = me
         for b in range(n.bit_length() - 1):
@@ -41,6 +43,21 @@
                 q = q + (1 - 2 * lax.rem(me // (1 << b), 2)) * (1 << b)
         return q, q
     return lax.rem(me + k, n), lax.rem(me + n - k, n)
+
+
+def slot(k):
+    return (k[0] if isinstance(k, tuple) else k) - 1
+
+
+def line(me, n, body):
+    if n != 4:
+        each(1, n, body)
+        return
+    upper = me // 2
+    inner = lax.rem((me + 1) // 2, 2)
+    body((3 - inner, 3 * (1 - upper)))
+    body((2 + inner, 2 - upper))
+    body(1)
 
 
 def kernel(
@@ -117,8 +134,8 @@
 
     def scatter(k, part, got, send, recv):
         return pltpu.make_async_remote_copy(
-            src_ref=part.at[partner(tower, k, towers)[0]], dst_ref=got.at[k - 1],
-            send_sem=send.at[k - 1], recv_sem=recv.at[k - 1],
+            src_ref=part.at[partner(tower, k, towers)[0]], dst_ref=got.at[slot(k)],
+            send_sem=send.at[slot(k)], recv_sem=recv.at[slot(k)],
             device_id=tower_at(k), device_id_type=MESH)
 
     load_lens.wait()
@@ -141,14 +158,14 @@
     load_wt.wait()
     encode(jnp.dot(pooled, wt[...], preferred_element_type=F32), flat_t, down_t, part_t, note_t)
     pl.semaphore_wait(barrier, towers + planes - 2)
-    each(1, towers, lambda k: scatter(k, note_t, told_t, s7, r7).start())
-    each(1, towers, lambda k: scatter(k, part_t, got_t, s1, r1).start())
+    line(tower, towers, lambda k: scatter(k, note_t, told_t, s7, r7).start())
+    line(tower, towers, lambda k: scatter(k, part_t, got_t, s1, r1).start())
 
     load_feats.wait()
     load_wi.wait()
     encode(jnp.dot(feats[...], wi[...], preferred_element_type=F32), flat_i, down_i, part_i, note_i)
-    each(1, towers, lambda k: scatter(k, note_i, told_i, s8, r8).start())
-    each(1, towers, lambda k: scatter(k, part_i, got_i, s2, r2).start())
+    line(tower, towers, lambda k: scatter(k, note_i, told_i, s8, r8).start())
+    line(tower, towers, lambda k: scatter(k, part_i, got_i, s2, r2).start())
 
     def unit(flat, down, part, got, send, recv, note, told, note_send, note_recv):
         raw = gather(flat, block(tower), sub) * down[pl.ds(tower * sub, sub), 0:1]
@@ -172,7 +189,7 @@
     def give_i(k):
         return pltpu.make_async_remote_copy(
             src_ref=images.at[tower], dst_ref=images.at[tower],
-            send_sem=s4.at[k - 1], recv_sem=r4.at[k - 1],
+            send_sem=s4.at[slot(k)], recv_sem=r4.at[slot(k)],
             device_id=tower_at(k), device_id_type=MESH)
 
     spread(full_t, block(plane), unit(
@@ -182,7 +199,7 @@
     spread(full_i, block(tower), unit(
         flat_i, down_i, part_i, got_i, s2, r2, note_i, told_i, s8, r8))
     images[tower, 0:rows, :] = full_i[pl.ds(block(tower), rows), :].astype(BF16)
-    each(1, towers, lambda k: give_i(k).start())
+    line(tower, towers, lambda k: give_i(k).start())
 
     def take_i(k):
         give_i(k).wait_recv()
@@ -211,8 +228,8 @@
 
     def back_image(k):
         return pltpu.make_async_remote_copy(
-            src_ref=term_i.at[partner(tower, k, towers)[0]], dst_ref=back_i.at[k - 1],
-            send_sem=s5.at[k - 1], recv_sem=r5.at[k - 1],
+            src_ref=term_i.at[partner(tower, k, towers)[0]], dst_ref=back_i.at[slot(k)],
+            send_sem=s5.at[slot(k)], recv_sem=r5.at[slot(k)],
             device_id=tower_at(k), device_id_type=MESH)
 
     def back_text(k):
@@ -227,7 +244,7 @@
 
     spread(sums_i, 0, jnp.dot(grads.astype(BF16), all_t, preferred_element_type=F32))
     stage(towers, sums_i, term_i)
-    each(1, towers, lambda k: back_image(k).start())
+    line(tower, towers, lambda k: back_image(k).start())
     spread(sums_t, 0, jnp.dot(grads.T.astype(BF16), all_i, preferred_element_type=F32))
     stage(planes, sums_t, term_t)
     each(1, planes, lambda k: back_text(k).start())

time: 22.3 us -> 22.1 us (level)
  no operation moved by 1% of the time
where the time goes in v6:
time: 22.1 us; the launch traced here: 21.9 us
  Pallas kernels  20 us (90%)
  between operations  1.93 us (9%)
    pallas_call x1, Pallas kernels, per_device(): pl.pallas_call(functools.partial(kernel, sub, towers, pipes, planes), out...  19.3 us
    pallas_call x1, Pallas kernels, per_device(): pl.pallas_call(finish, out_shape=(out, out), in_specs=[pl.BlockSpec(memor...  0.64 us

profile of v6, /device:TPU:0, one launch (start us, length us, event | category | flops | bytes accessed | tf_op | source)
XLA Modules:
  0.0 21.9 jit_solution(16479215895044546623)
XLA Ops:
  1.9 19.3 %shard_map.86 = (f32[6,1,1536]{2,1,0:T(1,128)S(1)}, f32[6,1,1536]{2,1,0:T(1,128)S(1)}) custom-call(f32[1]{0:T(128)S(6)} %copy.11.scale_hbm, f32[1]{0:T(128)S(6)} %copy.12.shift_hbm, bf16[1,1,24,384]{3,2,1,0:T(8,128)(2,1)} %feats_hbm.1, bf16[1,1,24,64,288]{4,3,2,1,0:T(8,128)(2,1)} %words_hbm.1, s32[1,1,24]{2,1,0:T(1,128)} %lens_hbm.1, ...), custom_call_target="tpu_custom_call" | custom-call | tf_op jit(solution)/shard_map/pallas_call | solution.py:294
  21.3 0.6 %shard_map.87 = (f32[6,1,1536]{2,1,0:T(1,128)}, f32[6,1,1536]{2,1,0:T(1,128)}) custom-call(f32[6,1,1536]{2,1,0:T(1,128)S(1)} %get-tuple-element.6.image_ref, f32[6,1,1536]{2,1,0:T(1,128)S(1)} %get-tuple-element.7.text_ref), custom_call_target="tpu_custom_call" | custom-call | tf_op jit(solution)/shard_map/pallas_call | solution.py:335

commit v7 on v6

--- a/solution.py
+++ b/solution.py
@@ -238,16 +238,21 @@
             send_sem=s6.at[k - 1], recv_sem=r6.at[k - 1],
             device_id=plane_at(k), device_id_type=MESH)
 
-    def stage(n, sums, term):
-        for d in range(n):
-            term[d, 0:rows, :] = sums[d * rows:(d + 1) * rows, :].astype(WIRE)
+    def stage(q, sums, term):
+        term[q, 0:rows, :] = sums[pl.ds(block(q), rows), :].astype(WIRE)
+
+    def return_image(k):
+        stage(partner(tower, k, towers)[0], sums_i, term_i)
+        back_image(k).start()
+
+    def return_text(k):
+        stage(partner(plane, k, planes)[0], sums_t, term_t)
+        back_text(k).start()
 
     spread(sums_i, 0, jnp.dot(grads.astype(BF16), all_t, preferred_element_type=F32))
-    stage(towers, sums_i, term_i)
-    line(tower, towers, lambda k: back_image(k).start())
+    line(tower, towers, return_image)
     spread(sums_t, 0, jnp.dot(grads.T.astype(BF16), all_i, preferred_element_type=F32))
-    stage(planes, sums_t, term_t)
-    each(1, planes, lambda k: back_text(k).start())
+    each(1, planes, return_text)
 
     def total(sums, me, back, wait, n, out):
         near(1, n, wait)

time: 22.1 us -> 22.1 us (level)
  no operation moved by 1% of the time
where the time goes in v7:
time: 22.1 us; the launch traced here: 21.9 us
  Pallas kernels  20 us (90%)
  between operations  1.93 us (9%)
    pallas_call x1, Pallas kernels, per_device(): pl.pallas_call(functools.partial(kernel, sub, towers, pipes, planes), out...  19.3 us
    pallas_call x1, Pallas kernels, per_device(): pl.pallas_call(finish, out_shape=(out, out), in_specs=[pl.BlockSpec(memor...  0.64 us

profile of v7, /device:TPU:0, one launch (start us, length us, event | category | flops | bytes accessed | tf_op | source)
XLA Modules:
  0.0 21.9 jit_solution(8352965631513092274)
XLA Ops:
  1.9 19.3 %shard_map.86 = (f32[6,1,1536]{2,1,0:T(1,128)S(1)}, f32[6,1,1536]{2,1,0:T(1,128)S(1)}) custom-call(f32[1]{0:T(128)S(6)} %copy.11.scale_hbm, f32[1]{0:T(128)S(6)} %copy.12.shift_hbm, bf16[1,1,24,384]{3,2,1,0:T(8,128)(2,1)} %feats_hbm.1, bf16[1,1,24,64,288]{4,3,2,1,0:T(8,128)(2,1)} %words_hbm.1, s32[1,1,24]{2,1,0:T(1,128)} %lens_hbm.1, ...), custom_call_target="tpu_custom_call" | custom-call | tf_op jit(solution)/shard_map/pallas_call | solution.py:299
  21.3 0.6 %shard_map.87 = (f32[6,1,1536]{2,1,0:T(1,128)}, f32[6,1,1536]{2,1,0:T(1,128)}) custom-call(f32[6,1,1536]{2,1,0:T(1,128)S(1)} %get-tuple-element.6.image_ref, f32[6,1,1536]{2,1,0:T(1,128)S(1)} %get-tuple-element.7.text_ref), custom_call_target="tpu_custom_call" | custom-call | tf_op jit(solution)/shard_map/pallas_call | solution.py:340

commit v8 on v6

--- a/solution.py
+++ b/solution.py
@@ -28,6 +28,14 @@
 def near(lo, hi, body):
     if hi - lo <= UNROLL:
         for k in sorted(range(lo, hi), key=lambda k: (bin(k).count("1"), k)):
+            body(k)
+    else:
+        each(lo, hi, body)
+
+
+def far(lo, hi, step, body):
+    if hi - lo <= UNROLL:
+        for k in sorted(range(lo, hi), key=lambda k: (-bin(k & ~step).count("1"), -k)):
             body(k)
     else:
         each(lo, hi, body)
@@ -195,7 +203,7 @@
     spread(full_t, block(plane), unit(
         flat_t, down_t, part_t, got_t, s1, r1, note_t, told_t, s7, r7))
     texts[plane, 0:rows, :] = full_t[pl.ds(block(plane), rows), :].astype(BF16)
-    each(1, planes, lambda k: give_t(k).start())
+    far(1, planes, pipes, lambda k: give_t(k).start())
     spread(full_i, block(tower), unit(
         flat_i, down_i, part_i, got_i, s2, r2, note_i, told_i, s8, r8))
     images[tower, 0:rows, :] = full_i[pl.ds(block(tower), rows), :].astype(BF16)
@@ -247,7 +255,7 @@
     line(tower, towers, lambda k: back_image(k).start())
     spread(sums_t, 0, jnp.dot(grads.T.astype(BF16), all_i, preferred_element_type=F32))
     stage(planes, sums_t, term_t)
-    each(1, planes, lambda k: back_text(k).start())
+    far(1, planes, pipes, lambda k: back_text(k).start())
 
     def total(sums, me, back, wait, n, out):
         near(1, n, wait)

time: 22.1 us -> 21.9 us (level)
  no operation moved by 1% of the time
where the time goes in v8:
time: 21.9 us; the launch traced here: 21.7 us
  Pallas kernels  19.8 us (90%)
  between operations  1.93 us (9%)
    pallas_call x1, Pallas kernels, per_device(): pl.pallas_call(functools.partial(kernel, sub, towers, pipes, planes), out...  19.1 us
    pallas_call x1, Pallas kernels, per_device(): pl.pallas_call(finish, out_shape=(out, out), in_specs=[pl.BlockSpec(memor...  0.64 us

profile of v8, /device:TPU:0, one launch (start us, length us, event | category | flops | bytes accessed | tf_op | source)
XLA Modules:
  0.0 21.7 jit_solution(13983704211492266322)
XLA Ops:
  1.9 19.1 %shard_map.86 = (f32[6,1,1536]{2,1,0:T(1,128)S(1)}, f32[6,1,1536]{2,1,0:T(1,128)S(1)}) custom-call(f32[1]{0:T(128)S(6)} %copy.11.scale_hbm, f32[1]{0:T(128)S(6)} %copy.12.shift_hbm, bf16[1,1,24,384]{3,2,1,0:T(8,128)(2,1)} %feats_hbm.1, bf16[1,1,24,64,288]{4,3,2,1,0:T(8,128)(2,1)} %words_hbm.1, s32[1,1,24]{2,1,0:T(1,128)} %lens_hbm.1, ...), custom_call_target="tpu_custom_call" | custom-call | tf_op jit(solution)/shard_map/pallas_call | solution.py:302
  21.1 0.6 %shard_map.87 = (f32[6,1,1536]{2,1,0:T(1,128)}, f32[6,1,1536]{2,1,0:T(1,128)}) custom-call(f32[6,1,1536]{2,1,0:T(1,128)S(1)} %get-tuple-element.6.image_ref, f32[6,1,1536]{2,1,0:T(1,128)S(1)} %get-tuple-element.7.text_ref), custom_call_target="tpu_custom_call" | custom-call | tf_op jit(solution)/shard_map/pallas_call | solution.py:343
